TPU v7x, 256 devices: a whole 4x4x8 slice. The times are simulated.
256 devices in a mesh: seq: 64 (over y, z_lo, x), mp: 4 (over z_hi, core).
Axes of the slice: x: 4, y: 4, z: 8 (z_hi: 2, z_lo: 4; z = z_hi * 4 + z_lo), core: 2. Of those that a mesh axis runs over, the one named last changes fastest.
Arguments:
- projected: bfloat16 [3, 8192, 8192], P(None, 'mp', 'seq'), may hold values from -6 to 6
- short_taps: float32 [3, 3, 8192], replicated, may hold values from -4 to 4
- skip_gain: float32 [8192], replicated, may hold values from -4 to 4
- residue: float32 [2048, 16], P('seq'), may hold values from -4 to 4
- decay_rate: float32 [2048, 16], P('seq'), may hold values from 6.1035156e-05 to 0.05
Outputs:
- gated: bfloat16 [8192, 8192], P('mp', 'seq')
All inputs are finite; a program needn't handle non-finite values.
Results may differ from a plain program's by a relative error of at most 0.012.
Values may be sent and summed in bfloat16 or wider, within the bound.
No kernel may reach another device: no remote copies, remote signals or barrier semaphores. Data moves between devices by JAX's collectives and lax.ppermute only.
A program may use at most 128 MiB of HBM per device.

v0:
```python
import math
import jax
import jax.numpy as jnp
from jax import lax
from jax.sharding import PartitionSpec as P

exact_mode = lax.Precision.HIGHEST
full_turn = 2.0 * math.pi


def unit_table(row_count, column_count, period):
    indices = lax.broadcasted_iota(jnp.int32, (row_count, column_count), 0) * lax.broadcasted_iota(
        jnp.int32, (row_count, column_count), 1
    )
    angles = -full_turn / period * (indices % period).astype(jnp.float32)
    return (jnp.cos(angles), jnp.sin(angles))


def dft_tables(length):
    padded_len = 2 * length
    narrow = padded_len // 128
    outer_table = unit_table(128, 128, 128)
    twiddle = unit_table(128, narrow, padded_len)
    inner_table = unit_table(narrow, narrow, narrow)
    return (outer_table, twiddle, inner_table)


def forward(signal, tables):
    outer_table, twiddle, inner_table = tables
    signal_count = signal.shape[0]
    narrow = inner_table[0].shape[0]
    blocks = signal.reshape(signal_count, 64, narrow)
    section_re = jnp.einsum("ca,mab->mcb", outer_table[0][:, :64], blocks, precision=exact_mode)
    section_im = jnp.einsum("ca,mab->mcb", outer_table[1][:, :64], blocks, precision=exact_mode)
    turned_re = section_re * twiddle[0] - section_im * twiddle[1]
    turned_im = section_re * twiddle[1] + section_im * twiddle[0]
    spec_re = jnp.einsum(
        "mcb,bd->mcd", turned_re, inner_table[0], precision=exact_mode
    ) - jnp.einsum("mcb,bd->mcd", turned_im, inner_table[1], precision=exact_mode)
    spec_im = jnp.einsum(
        "mcb,bd->mcd", turned_re, inner_table[1], precision=exact_mode
    ) + jnp.einsum("mcb,bd->mcd", turned_im, inner_table[0], precision=exact_mode)
    return (spec_re, spec_im)


def inverse(spec_re, spec_im, tables):
    outer_table, twiddle, inner_table = tables
    signal_count = spec_re.shape[0]
    narrow = inner_table[0].shape[0]
    back_re = jnp.einsum("mcd,bd->mcb", spec_re, inner_table[0], precision=exact_mode) + jnp.einsum(
        "mcd,bd->mcb", spec_im, inner_table[1], precision=exact_mode
    )
    back_im = jnp.einsum("mcd,bd->mcb", spec_im, inner_table[0], precision=exact_mode) - jnp.einsum(
        "mcd,bd->mcb", spec_re, inner_table[1], precision=exact_mode
    )
    turned_re = back_re * twiddle[0] + back_im * twiddle[1]
    turned_im = back_im * twiddle[0] - back_re * twiddle[1]
    result = jnp.einsum(
        "ca,mcb->mab", outer_table[0][:, :64], turned_re, precision=exact_mode
    ) + jnp.einsum("ca,mcb->mab", outer_table[1][:, :64], turned_im, precision=exact_mode)
    return result.reshape(signal_count, 64 * narrow) / (128.0 * narrow)


def filter_kernel(residue, decay_rate, length):
    positions = lax.broadcasted_iota(jnp.float32, (1, length), 1)

    def add_term(state_index, kernel):
        rates = lax.dynamic_slice_in_dim(decay_rate, state_index, 1, 1)
        weight = lax.dynamic_slice_in_dim(residue, state_index, 1, 1) * jnp.sqrt(rates)
        return kernel + weight * jnp.exp(-rates * positions)

    return lax.fori_loop(
        0, residue.shape[1], add_term, jnp.zeros((residue.shape[0], length), jnp.float32)
    )


def long_convolve(product, residue, decay_rate):
    signal_count, length = product.shape
    tables = dft_tables(length)
    signal_re, signal_im = forward(product.astype(jnp.float32), tables)
    mp_count = lax.axis_size("mp")
    per_group = signal_count // mp_count
    local_residue = lax.dynamic_slice_in_dim(
        residue, lax.axis_index("mp") * per_group, per_group, 0
    )
    local_rate = lax.dynamic_slice_in_dim(
        decay_rate, lax.axis_index("mp") * per_group, per_group, 0
    )
    kernel_re, kernel_im = forward(filter_kernel(local_residue, local_rate, length), tables)
    grouped_shape = (mp_count, per_group) + signal_re.shape[1:]
    signal_re = signal_re.reshape(grouped_shape)
    signal_im = signal_im.reshape(grouped_shape)
    kernel_re = kernel_re[None]
    kernel_im = kernel_im[None]
    mixed_re = (signal_re * kernel_re - signal_im * kernel_im).reshape(
        (signal_count,) + signal_re.shape[-2:]
    )
    mixed_im = (signal_re * kernel_im + signal_im * kernel_re).reshape(
        (signal_count,) + signal_re.shape[-2:]
    )
    return inverse(mixed_re, mixed_im, tables).astype(jnp.bfloat16)


def to_channels(streams):
    stream_count, chan_width, row_count = streams.shape
    seq_count = lax.axis_size("seq")
    mp_count = lax.axis_size("mp")
    arranged = streams.reshape(
        stream_count, seq_count, mp_count, chan_width // (seq_count * mp_count), row_count
    )
    arrived = lax.all_to_all(
        lax.all_to_all(arranged, "seq", split_axis=1, concat_axis=4, tiled=True),
        "mp",
        split_axis=2,
        concat_axis=2,
        tiled=True,
    )
    return arrived.reshape(stream_count, chan_width // seq_count, row_count * seq_count)


def from_channels(values):
    chan_dev, length = values.shape
    seq_count = lax.axis_size("seq")
    mp_count = lax.axis_size("mp")
    arranged = values.reshape(1, mp_count, chan_dev // mp_count, length)
    arrived = lax.all_to_all(
        lax.all_to_all(arranged, "seq", split_axis=3, concat_axis=0, tiled=True),
        "mp",
        split_axis=1,
        concat_axis=1,
        tiled=True,
    )
    return arrived.reshape(seq_count * chan_dev, length // seq_count)


def chosen_channels(full, chan_dev, chan_width):
    model_index = lax.axis_index("mp")
    seq_index = lax.axis_index("seq")
    mp_count = lax.axis_size("mp")
    piece_size = chan_dev // mp_count
    grouped = full.reshape(full.shape[:-1] + (mp_count, chan_width))
    selected = lax.dynamic_slice_in_dim(
        grouped, seq_index * chan_dev + model_index * piece_size, piece_size, grouped.ndim - 1
    )
    return selected.reshape(full.shape[:-1] + (chan_dev,))


def short_convolve(extended, tap_block):
    return (
        tap_block[0][:, :, None] * extended[:, :, 2:]
        + tap_block[1][:, :, None] * extended[:, :, 1:-1]
        + tap_block[2][:, :, None] * extended[:, :, :-2]
    )


def body(projected, short_taps, skip_gain, residue, decay_rate):
    chan_width = projected.shape[1]
    chan_dev = chan_width // lax.axis_size("seq")
    streams = to_channels(projected)
    taps_here = chosen_channels(short_taps, chan_dev, chan_width)
    skip_here = chosen_channels(skip_gain, chan_dev, chan_width)
    extended = jnp.pad(streams.astype(jnp.float32), ((0, 0), (0, 0), (2, 0)))
    mixed = short_convolve(extended, taps_here)
    product = (mixed[1] * mixed[2]).astype(jnp.bfloat16)
    long_part = long_convolve(product, residue, decay_rate)
    total = long_part.astype(jnp.float32) + skip_here[:, None] * product.astype(jnp.float32)
    return from_channels((mixed[0] * total).astype(jnp.bfloat16))


def solution(mesh):
    in_specs = (P(None, "mp", "seq"), P(), P(), P("seq", None), P("seq", None))
    out_specs = P("mp", "seq")
    return jax.shard_map(body, mesh=mesh, in_specs=in_specs, out_specs=out_specs, check_vma=False)
```

profile of v0, /device:TPU:33, one launch (start us, length us, event | category | flops | bytes accessed | tf_op | source)
XLA Modules:
  0.0 227.2 jit_solution(2267840420173184764)
XLA Ops:
  0.0 2.8 %copy.98 = bf16[3,64,4,8,128]{4,3,2,0,1:T(8,128)(2,1)} copy(bf16[3,64,4,8,128]{4,3,2,1,0:T(8,128)(2,1)} %bitcast.146) | data formatting | bytes 3145728 | tf_op jit(solution)/shard_map/reshape | solution.py:108
  2.8 11.2 %all-to-all-start = ((bf16[3,64,4,8,128]{4,3,2,0,1:T(8,128)(2,1)}), bf16[3,64,4,8,128]{4,3,2,0,1:T(8,128)(2,1)S(1)}, u32[]{:S(2)}, u32[]{:S(2)}) async-start(bf16[3,64,4,8,128]{4,3,2,0,1:T(8,128)(2,1)} %copy.98), calls=%async_computation | async-start | bytes 3145728 | tf_op jit(solution)/shard_map/all_to_all | solution.py:112
  14.2 36.9 %all-to-all-done = bf16[3,64,4,8,128]{4,3,2,0,1:T(8,128)(2,1)S(1)} async-done(((bf16[3,64,4,8,128]{4,3,2,0,1:T(8,128)(2,1)}), bf16[3,64,4,8,128]{4,3,2,0,1:T(8,128)(2,1)S(1)}, u32[]{:S(2)}, u32[]{:S(2)}) %all-to-all-start) | async-done | bytes 1572896 | tf_op jit(solution)/shard_map/all_to_all | solution.py:112
  51.1 0.6 copy.159
  51.7 2.1 reshape.166
  53.8 7.2 %all-to-all-start.1 = ((bf16[3,1,4,8,8192]{4,3,0,1,2:T(8,128)(2,1)}), bf16[3,1,4,8,8192]{4,3,0,1,2:T(8,128)(2,1)S(1)}, u32[]{:S(2)}, u32[]{:S(2)}) async-start(bf16[3,1,4,8,8192]{4,3,0,1,2:T(8,128)(2,1)} %reshape.166), calls=%async_computation.1 | async-start | bytes 3145728 | tf_op jit(solution)/shard_map/all_to_all | solution.py:111
  61.0 3.3 %while.14 = (s32[]{:T(128)}, f32[8,8192]{1,0:T(8,128)S(1)}, f32[8,16]{0,1:T(8,128)S(1)}, f32[8,16]{0,1:T(8,128)S(1)}, s32[]{:T(128)}, /*index=5*/s32[]{:T(128)}) while((s32[]{:T(128)}, f32[8,8192]{1,0:T(8,128)S(1)}, f32[8,16]{0,1:T(8,128)S(1)}, f32[8,16]{0,1:T(8,128)S(1)}, s32[]{:T(128)}, /*index=5*/s32[]{:T(128)}) %tuple.40), condition=%wide.region_1.2_spmd.clone, body=%wide.region_0.1_spmd.clone.sunk | while | flops 262163 | bytes 524571 | solution.py:72
  61.0 0.1 fusion.149
  61.2 0.1 fusion.149
  61.9 0.1 fusion.149
  62.1 0.1 fusion.149
  63.0 0.1 fusion.149
  63.1 0.1 fusion.149
  63.3 0.1 fusion.149
  64.3 0.3 reshape.144
  65.1 0.3 fusion.77
  65.3 0.3 fusion.78
  65.6 0.3 fusion.75
  65.9 1.0 convolution_bitcast_fusion
  66.9 1.0 convolution_bitcast_fusion.1
  67.9 1.2 fusion.48
  69.1 1.2 fusion.49
  70.3 2.0 convolution_add_fusion.2
  72.3 2.0 convolution_subtract_fusion.2
  74.3 26.5 %all-to-all-done.1 = bf16[3,1,4,8,8192]{4,3,0,1,2:T(8,128)(2,1)S(1)} async-done(((bf16[3,1,4,8,8192]{4,3,0,1,2:T(8,128)(2,1)}), bf16[3,1,4,8,8192]{4,3,0,1,2:T(8,128)(2,1)S(1)}, u32[]{:S(2)}, u32[]{:S(2)}) %all-to-all-start.1) | async-done | bytes 1572896 | tf_op jit(solution)/shard_map/all_to_all | solution.py:111
  100.9 0.3 bitcast_convert_fusion
  101.2 1.7 multiply_add_fusion
  103.1 1.2 fusion.92
  104.4 1.4 fusion.91
  105.7 3.6 %fusion.44 = f32[32,128,128]{2,1,0:T(8,128)S(1)} fusion(f32[32,128,128]{2,1,0:T(8,128)S(1)} %fusion.92, f32[32,128,128]{2,1,0:T(8,128)S(1)} %fusion.91, f32[128,128]{0,1:T(8,128)S(1)} %get-tuple-element.132, f32[128,128]{0,1:T(8,128)S(1)} %get-tuple-element.133), kind=kOutput, calls=%fused_computation.55 | convolution fusion | flops 807108608 | bytes 6422528 | tf_op jit(solution)/shard_map/mcb,bd->mcd/dot_general | solution.py:37
  109.4 3.6 %fusion.42 = f32[32,128,128]{2,1,0:T(8,128)S(1)} fusion(f32[32,128,128]{2,1,0:T(8,128)S(1)} %fusion.92, f32[32,128,128]{2,1,0:T(8,128)S(1)} %fusion.91, f32[128,128]{0,1:T(8,128)S(1)} %get-tuple-element.132, f32[128,128]{0,1:T(8,128)S(1)} %get-tuple-element.133), kind=kOutput, calls=%fused_computation.54 | convolution fusion | flops 807108608 | bytes 6422528 | tf_op jit(solution)/shard_map/mcb,bd->mcd/dot_general | solution.py:40
  113.0 3.6 %convolution_subtract_fusion.1 = f32[32,128,128]{2,1,0:T(8,128)S(1)} fusion(f32[32,128,128]{2,1,0:T(8,128)S(1)} %fusion.44, f32[32,128,128]{2,1,0:T(8,128)S(1)} %fusion.92, f32[32,128,128]{2,1,0:T(8,128)S(1)} %fusion.91, f32[128,128]{0,1:T(8,128)S(1)} %get-tuple-element.132, f32[128,128]{0,1:T(8,128)S(1)} %get-tuple-element.133), kind=kOutput, calls=%fused_computation.32 | convolution fusion | flops 807632896 | bytes 8519680 | tf_op jit(solution)/shard_map/mcb,bd->mcd/dot_general | solution.py:39
  116.7 4.0 %fusion.6 = (f32[32,128,128]{2,1,0:T(8,128)S(1)}, f32[32,128,128]{2,1,0:T(8,128)S(1)}) fusion(f32[32,128,128]{2,1,0:T(8,128)S(1)} %convolution_subtract_fusion.1, f32[8,128,128]{2,1,0:T(8,128)S(1)} %copy-done, f32[8,128,128]{2,1,0:T(8,128)S(1)} %copy-done.1, f32[32,128,128]{2,1,0:T(8,128)S(1)} %fusion.42, f32[32,128,128]{2,1,0:T(8,128)S(1)} %fusion.92, ...), kind=kOutput, calls=%fused_computation.14 | convolution fusion | flops 810778624 | bytes 13762560 | tf_op jit(solution)/shard_map/mcb,bd->mcd/dot_general | solution.py:42
  120.7 2.3 fusion.62
  123.0 2.3 %fusion.60 = f32[32,128,128]{1,2,0:T(8,128)S(1)} fusion(f32[32,128,128]{2,1,0:T(8,128)S(1)} %get-tuple-element.127), kind=kOutput, calls=%fused_computation.77 | convolution fusion | flops 805535744 | bytes 4194304 | tf_op jit(solution)/shard_map/mcd,bd->mcb/dot_general | solution.py:53
  125.3 2.3 convolution_add_fusion
  127.5 2.5 %convolution_subtract_fusion = f32[32,128,128]{1,2,0:T(8,128)S(1)} fusion(f32[32,128,128]{1,2,0:T(8,128)S(1)} %fusion.60, f32[32,128,128]{2,1,0:T(8,128)S(1)} %get-tuple-element.128), kind=kOutput, calls=%fused_computation.29 | convolution fusion | flops 806060032 | bytes 6291456 | tf_op jit(solution)/shard_map/mcd,bd->mcb/dot_general | solution.py:53
  130.1 2.6 %fusion.9 = f32[32,128,64]{1,2,0:T(8,128)S(1)} fusion(f32[32,128,128]{1,2,0:T(8,128)S(1)} %convolution_add_fusion, f32[32,128,128]{1,2,0:T(8,128)S(1)} %convolution_subtract_fusion, f32[128,128]{0,1:T(8,128)S(1)} %get-tuple-element.132, f32[128,128]{0,1:T(8,128)S(1)} %get-tuple-element.133, f32[128,128]{0,1:T(8,128)S(1)} %fusion.77), kind=kOutput, calls=%fused_computation.21 | convolution fusion | flops 404226048 | bytes 5406720 | tf_op jit(solution)/shard_map/ca,mcb->mab/dot_general | solution.py:60
  132.7 3.6 %fusion.29 = f32[32,64,128]{2,1,0:T(8,128)} fusion(f32[32,128,64]{1,2,0:T(8,128)S(1)} %fusion.9, f32[32,128,128]{1,2,0:T(8,128)S(1)} %convolution_subtract_fusion, f32[32,128,128]{1,2,0:T(8,128)S(1)} %convolution_add_fusion, f32[128,128]{0,1:T(8,128)S(1)} %get-tuple-element.132, f32[128,128]{0,1:T(8,128)S(1)} %get-tuple-element.133, f32[128,128]{0,1:T(8,128)S(1)} %fusion.78), kind=kOutput, calls=%fused_computation.38 | convolution fusion | flops 405274624 | bytes 6455296 | tf_op jit(solution)/shard_map/ca,mcb->mab/dot_general | solution.py:58
  136.4 2.4 %reshape.150 = f32[1,4,8,8192]{3,2,1,0:T(8,128)} reshape(f32[32,64,128]{2,1,0:T(8,128)} %fusion.29) | data formatting | bytes 2097152 | tf_op jit(solution)/shard_map/convert_element_type | solution.py:166
  138.8 2.2 fusion.34
  141.0 9.6 %copy.130 = bf16[1,4,8,8192]{2,1,0,3:T(4,128)(2,1)} copy(bf16[1,4,8,8192]{3,2,1,0:T(8,128)(2,1)} %fusion.34) | data formatting | bytes 1048576 | tf_op jit(solution)/shard_map/convert_element_type | solution.py:167
  150.6 10.5 %reshape.167 = bf16[64,2,2048]{2,1,0:T(2,128)(2,1)S(1)} reshape(bf16[8192,1,4,8]{3,2,1,0:T(4,128)(2,1)} %bitcast.138) | data formatting | bytes 1048576
  161.1 20.9 %all_to_all.46 = bf16[64,2,2048]{2,1,0:T(2,128)(2,1)S(1)} all-to-all(bf16[64,2,2048]{2,1,0:T(2,128)(2,1)S(1)} %reshape.167), channel_id=1, replica_groups=mesh['seq'=64,'mp'=4] {'seq'}, dimensions={0} | all-to-all | bytes 1048576 | tf_op jit(solution)/shard_map/all_to_all | solution.py:127
  182.0 10.9 %reshape.168 = bf16[8192,1,4,8]{3,2,1,0:T(4,128)(2,1)} reshape(bf16[64,2,2048]{2,1,0:T(2,128)(2,1)S(1)} %all_to_all.46) | data formatting | bytes 1048576
  192.9 9.9 %copy.131 = bf16[1,4,8,64,128]{4,2,3,1,0:T(8,128)(2,1)S(1)} copy(bf16[1,4,8,64,128]{2,1,4,3,0:T(4,128)(2,1)} %bitcast.139) | data formatting | bytes 1048576 | tf_op jit(solution)/shard_map/all_to_all | solution.py:127
  202.8 23.2 %all_to_all.47 = bf16[64,4,8,128]{3,2,0,1:T(8,128)(2,1)S(1)} all-to-all(bf16[64,4,8,128]{3,2,0,1:T(8,128)(2,1)S(1)} %bitcast.145), channel_id=1, replica_groups=mesh['seq'=64,'mp'=4] {'mp'}, dimensions={1} | all-to-all | bytes 1048576 | tf_op jit(solution)/shard_map/all_to_all | solution.py:126
  226.0 0.9 copy.132
  (47 shorter events, 2.1 us)
Async XLA Ops:
  2.8 11.3 %copy-start.4 = (f32[32,16]{0,1:T(8,128)S(1)}, f32[32,16]{0,1:T(8,128)}, u32[]{:S(2)}) copy-start(f32[32,16]{0,1:T(8,128)} %param.11) | copy-start | bytes 6148
  2.8 11.3 %copy-start.5 = (f32[32,16]{0,1:T(8,128)S(1)}, f32[32,16]{0,1:T(8,128)}, u32[]{:S(2)}) copy-start(f32[32,16]{0,1:T(8,128)} %param.10) | copy-start | bytes 6148
  2.8 48.3 %all-to-all-start = ((bf16[3,64,4,8,128]{4,3,2,0,1:T(8,128)(2,1)}), bf16[3,64,4,8,128]{4,3,2,0,1:T(8,128)(2,1)S(1)}, u32[]{:S(2)}, u32[]{:S(2)}) async-start(bf16[3,64,4,8,128]{4,3,2,0,1:T(8,128)(2,1)} %copy.98), calls=%async_computation | async-start | bytes 3145728 | tf_op jit(solution)/shard_map/all_to_all | solution.py:112
  53.8 47.1 %all-to-all-start.1 = ((bf16[3,1,4,8,8192]{4,3,0,1,2:T(8,128)(2,1)}), bf16[3,1,4,8,8192]{4,3,0,1,2:T(8,128)(2,1)S(1)}, u32[]{:S(2)}, u32[]{:S(2)}) async-start(bf16[3,1,4,8,8192]{4,3,0,1,2:T(8,128)(2,1)} %reshape.166), calls=%async_computation.1 | async-start | bytes 3145728 | tf_op jit(solution)/shard_map/all_to_all | solution.py:111
  61.0 3.3 %copy-start.2 = (f32[3,3,8192]{2,1,0:T(4,128)S(1)}, f32[3,3,8192]{2,1,0:T(4,128)}, u32[]{:S(2)}) copy-start(f32[3,3,8192]{2,1,0:T(4,128)} %param.8) | copy-start | bytes 884740
  61.0 3.9 %copy-start.3 = (f32[8192]{0:T(1024)S(1)}, f32[8192]{0:T(1024)}, u32[]{:S(2)}) copy-start(f32[8192]{0:T(1024)} %param.9) | copy-start | bytes 98308
  113.0 3.7 %copy-start = (f32[8,128,128]{2,1,0:T(8,128)S(1)}, f32[8,128,128]{2,1,0:T(8,128)}, u32[]{:S(2)}) copy-start(f32[8,128,128]{2,1,0:T(8,128)} %convolution_add_fusion.2) | copy-start | bytes 1572868
  113.0 3.7 %copy-start.1 = (f32[8,128,128]{2,1,0:T(8,128)S(1)}, f32[8,128,128]{2,1,0:T(8,128)}, u32[]{:S(2)}) copy-start(f32[8,128,128]{2,1,0:T(8,128)} %convolution_subtract_fusion.2) | copy-start | bytes 1572868
where the time goes:
time: 231 us; the launch traced here: 227 us
  waiting for transfers between devices  63.5 us (27%)
  local copies, waits for them, and re-layouts  50.6 us (22%)
  blocking collectives  44.1 us (19%)
  matrix products  41.5 us (18%)
  starting transfers between devices  18.4 us (8%)
  other arithmetic  7.44 us (3%)
    all_to_all x1, waiting for transfers between devices, to_channels(): lax.all_to_all(arranged, 'seq', split_axis=1, concat_axis=4, tiled=True)  36.9 us
    all_to_all x1, waiting for transfers between devices, to_channels(): lax.all_to_all(lax.all_to_all(arranged, 'seq', split_axis=1, concat_axis=...  26.5 us
    all_to_all x1, blocking collectives, from_channels(): lax.all_to_all(lax.all_to_all(arranged, 'seq', split_axis=3, concat_axis=...  23.2 us
    unnamed x15, local copies, waits for them, and re-layouts  21.5 us
    all_to_all x1, blocking collectives, from_channels(): lax.all_to_all(arranged, 'seq', split_axis=3, concat_axis=0, tiled=True)  20.9 us
    all_to_all x1, starting transfers between devices, to_channels(): lax.all_to_all(arranged, 'seq', split_axis=1, concat_axis=4, tiled=True)  11.2 us
    all_to_all x1, local copies, waits for them, and re-layouts, from_channels(): lax.all_to_all(arranged, 'seq', split_axis=3, concat_axis=0, tiled=True)  9.86 us
    convert_element_type x1, local copies, waits for them, and re-layouts, body(): return from_channels((mixed[0] * total).astype(jnp.bfloat16))  9.63 us
  transfers between devices with their start and end apart: 2, of which 2 were waited for; matrix products, arithmetic and copies ran while one was open for 5% of the time, Pallas kernels for 0%

commit v1 on v0

--- a/solution.py
+++ b/solution.py
@@ -124,7 +124,12 @@
     mp_count = lax.axis_size("mp")
     arranged = values.reshape(1, mp_count, chan_dev // mp_count, length)
     arrived = lax.all_to_all(
-        lax.all_to_all(arranged, "seq", split_axis=3, concat_axis=0, tiled=True),
+        jnp.concatenate(
+            lax.all_to_all(
+                jnp.stack(jnp.split(arranged, lax.axis_size("seq"), axis=3)), "seq", 0, 0
+            ),
+            axis=0,
+        ),
         "mp",
         split_axis=1,
         concat_axis=1,

time: 231 us -> 189 us (0.82)
  local copies, waits for them, and re-layouts: 50.6 us -> 10.6 us
    unnamed x15 -> x76, local copies, waits for them, and re-layouts: 21.5 us -> 0.86 us
    all_to_all x2 -> x1, local copies, waits for them, and re-layouts: 10.7 us -> 0.88 us  [from_channels(): lax.all_to_all(jnp.concatenate(lax.all_to_all(jnp.stack(jnp.split(arrange...]
    convert_element_type x1 -> x0, local copies, waits for them, and re-layouts: 9.63 us -> none  [body(): return from_channels((mixed[0] * total).astype(jnp.bfloat16))]
  transfers between devices with their start and end apart: 2 -> 2, of which waited for: 2 -> 2; matrix products, arithmetic and copies ran while one was open for 5% -> 7% of each run, Pallas kernels for 0% -> 0%
where the time goes in v1:
time: 189 us; the launch traced here: 187 us
  waiting for transfers between devices  63.5 us (34%)
  blocking collectives  44.1 us (23%)
  matrix products  41.5 us (22%)
  starting transfers between devices  18.4 us (10%)
  local copies, waits for them, and re-layouts  10.6 us (6%)
  other arithmetic  6.65 us (4%)
    all_to_all x1, waiting for transfers between devices, to_channels(): lax.all_to_all(arranged, 'seq', split_axis=1, concat_axis=4, tiled=True)  36.9 us
    all_to_all x1, waiting for transfers between devices, to_channels(): lax.all_to_all(lax.all_to_all(arranged, 'seq', split_axis=1, concat_axis=...  26.5 us
    all_to_all x1, blocking collectives, from_channels(): lax.all_to_all(jnp.concatenate(lax.all_to_all(jnp.stack(jnp.split(arrange...  23.2 us
    all_to_all x1, blocking collectives, from_channels(): lax.all_to_all(jnp.stack(jnp.split(arranged, lax.axis_size('seq'), axis=3...  20.9 us
    all_to_all x1, starting transfers between devices, to_channels(): lax.all_to_all(arranged, 'seq', split_axis=1, concat_axis=4, tiled=True)  11.2 us
    all_to_all x1, starting transfers between devices, to_channels(): lax.all_to_all(lax.all_to_all(arranged, 'seq', split_axis=1, concat_axis=...  7.21 us
    dot_general x2, matrix products, forward(): jnp.einsum('mcb,bd->mcd', turned_im, inner_table[0], precision=exact_mode)  6 us
    dot_general x2, matrix products, forward(): jnp.einsum('mcb,bd->mcd', turned_im, inner_table[1], precision=exact_mode)  5.66 us
  transfers between devices with their start and end apart: 2, of which 2 were waited for; matrix products, arithmetic and copies ran while one was open for 7% of the time, Pallas kernels for 0%

profile of v1, /device:TPU:33, one launch (start us, length us, event | category | flops | bytes accessed | tf_op | source)
XLA Modules:
  0.0 186.6 jit_solution(9444098533070855559)
XLA Ops:
  0.0 2.8 %copy.252 = bf16[3,64,4,8,128]{4,3,2,0,1:T(8,128)(2,1)} copy(bf16[3,64,4,8,128]{4,3,2,1,0:T(8,128)(2,1)} %bitcast.395) | data formatting | bytes 3145728 | tf_op jit(solution)/shard_map/reshape | solution.py:108
  2.8 11.2 %all-to-all-start = ((bf16[3,64,4,8,128]{4,3,2,0,1:T(8,128)(2,1)}), bf16[3,64,4,8,128]{4,3,2,0,1:T(8,128)(2,1)S(1)}, u32[]{:S(2)}, u32[]{:S(2)}) async-start(bf16[3,64,4,8,128]{4,3,2,0,1:T(8,128)(2,1)} %copy.252), calls=%async_computation | async-start | bytes 3145728 | tf_op jit(solution)/shard_map/all_to_all | solution.py:112
  14.2 36.9 %all-to-all-done = bf16[3,64,4,8,128]{4,3,2,0,1:T(8,128)(2,1)S(1)} async-done(((bf16[3,64,4,8,128]{4,3,2,0,1:T(8,128)(2,1)}), bf16[3,64,4,8,128]{4,3,2,0,1:T(8,128)(2,1)S(1)}, u32[]{:S(2)}, u32[]{:S(2)}) %all-to-all-start) | async-done | bytes 1572896 | tf_op jit(solution)/shard_map/all_to_all | solution.py:112
  51.1 0.6 copy.312
  51.7 2.1 %reshape.170 = bf16[3,1,4,8,8192]{4,3,0,1,2:T(8,128)(2,1)} reshape(bf16[3,1,4,8,64,128]{5,4,3,0,2,1:T(8,128)(2,1)S(1)} %copy.312) | data formatting | bytes 3145728 | tf_op jit(solution)/shard_map/all_to_all | solution.py:112
  53.8 7.2 %all-to-all-start.1 = ((bf16[3,1,4,8,8192]{4,3,0,1,2:T(8,128)(2,1)}), bf16[3,1,4,8,8192]{4,3,0,1,2:T(8,128)(2,1)S(1)}, u32[]{:S(2)}, u32[]{:S(2)}) async-start(bf16[3,1,4,8,8192]{4,3,0,1,2:T(8,128)(2,1)} %reshape.170), calls=%async_computation.1 | async-start | bytes 3145728 | tf_op jit(solution)/shard_map/all_to_all | solution.py:111
  61.0 3.3 %while.14 = (s32[]{:T(128)}, f32[8,8192]{1,0:T(8,128)S(1)}, f32[8,16]{0,1:T(8,128)S(1)}, f32[8,16]{0,1:T(8,128)S(1)}, s32[]{:T(128)}, /*index=5*/s32[]{:T(128)}) while((s32[]{:T(128)}, f32[8,8192]{1,0:T(8,128)S(1)}, f32[8,16]{0,1:T(8,128)S(1)}, f32[8,16]{0,1:T(8,128)S(1)}, s32[]{:T(128)}, /*index=5*/s32[]{:T(128)}) %tuple.40), condition=%wide.region_1.2_spmd.clone, body=%wide.region_0.1_spmd.clone.sunk | while | flops 262163 | bytes 524571 | solution.py:72
  61.0 0.1 fusion.149
  61.2 0.1 fusion.149
  61.4 0.1 fusion.149
  61.6 0.1 fusion.149
  61.7 0.1 fusion.149
  61.9 0.1 fusion.149
  62.1 0.1 fusion.149
  62.3 0.1 fusion.149
  63.0 0.1 fusion.149
  63.1 0.1 fusion.149
  63.3 0.1 fusion.149
  64.3 0.3 reshape.147
  65.1 0.3 fusion.77
  65.3 0.3 fusion.78
  65.6 0.3 fusion.75
  65.9 1.0 convolution_bitcast_fusion
  66.9 1.0 convolution_bitcast_fusion.1
  67.9 1.2 fusion.48
  69.1 1.2 fusion.49
  70.3 2.0 %convolution_add_fusion.2 = f32[8,128,128]{2,1,0:T(8,128)} fusion(f32[8,128,128]{2,1,0:T(8,128)S(1)} %fusion.48, f32[8,128,128]{1,2,0:T(8,128)S(1)} %convolution_bitcast_fusion, f32[8,128,128]{1,2,0:T(8,128)S(1)} %convolution_bitcast_fusion.1, f32[128,128]{0,1:T(8,128)S(1)} %get-tuple-element.132, f32[128,128]{0,1:T(8,128)S(1)} %get-tuple-element.133), kind=kOutput, calls=%fused_computation.41 | convolution fusion | flops 202080256 | bytes 2228224 | tf_op jit(solution)/shard_map/mcb,bd->mcd/dot_general | solution.py:42
  72.3 2.0 %convolution_subtract_fusion.2 = f32[8,128,128]{2,1,0:T(8,128)} fusion(f32[8,128,128]{2,1,0:T(8,128)S(1)} %fusion.49, f32[8,128,128]{1,2,0:T(8,128)S(1)} %convolution_bitcast_fusion, f32[8,128,128]{1,2,0:T(8,128)S(1)} %convolution_bitcast_fusion.1, f32[128,128]{0,1:T(8,128)S(1)} %get-tuple-element.132, f32[128,128]{0,1:T(8,128)S(1)} %get-tuple-element.133), kind=kOutput, calls=%fused_computation.42 | convolution fusion | flops 202080256 | bytes 2228224 | tf_op jit(solution)/shard_map/mcb,bd->mcd/dot_general | solution.py:39
  74.3 26.5 %all-to-all-done.1 = bf16[3,1,4,8,8192]{4,3,0,1,2:T(8,128)(2,1)S(1)} async-done(((bf16[3,1,4,8,8192]{4,3,0,1,2:T(8,128)(2,1)}), bf16[3,1,4,8,8192]{4,3,0,1,2:T(8,128)(2,1)S(1)}, u32[]{:S(2)}, u32[]{:S(2)}) %all-to-all-start.1) | async-done | bytes 1572896 | tf_op jit(solution)/shard_map/all_to_all | solution.py:111
  100.9 0.3 bitcast_convert_fusion
  101.2 1.7 multiply_add_fusion
  103.1 1.2 fusion.92
  104.4 1.4 fusion.91
  105.7 3.6 %fusion.44 = f32[32,128,128]{2,1,0:T(8,128)S(1)} fusion(f32[32,128,128]{2,1,0:T(8,128)S(1)} %fusion.92, f32[32,128,128]{2,1,0:T(8,128)S(1)} %fusion.91, f32[128,128]{0,1:T(8,128)S(1)} %get-tuple-element.132, f32[128,128]{0,1:T(8,128)S(1)} %get-tuple-element.133), kind=kOutput, calls=%fused_computation.55 | convolution fusion | flops 807108608 | bytes 6422528 | tf_op jit(solution)/shard_map/mcb,bd->mcd/dot_general | solution.py:37
  109.4 3.6 %fusion.42 = f32[32,128,128]{2,1,0:T(8,128)S(1)} fusion(f32[32,128,128]{2,1,0:T(8,128)S(1)} %fusion.92, f32[32,128,128]{2,1,0:T(8,128)S(1)} %fusion.91, f32[128,128]{0,1:T(8,128)S(1)} %get-tuple-element.132, f32[128,128]{0,1:T(8,128)S(1)} %get-tuple-element.133), kind=kOutput, calls=%fused_computation.54 | convolution fusion | flops 807108608 | bytes 6422528 | tf_op jit(solution)/shard_map/mcb,bd->mcd/dot_general | solution.py:40
  113.0 3.6 %convolution_subtract_fusion.1 = f32[32,128,128]{2,1,0:T(8,128)S(1)} fusion(f32[32,128,128]{2,1,0:T(8,128)S(1)} %fusion.44, f32[32,128,128]{2,1,0:T(8,128)S(1)} %fusion.92, f32[32,128,128]{2,1,0:T(8,128)S(1)} %fusion.91, f32[128,128]{0,1:T(8,128)S(1)} %get-tuple-element.132, f32[128,128]{0,1:T(8,128)S(1)} %get-tuple-element.133), kind=kOutput, calls=%fused_computation.32 | convolution fusion | flops 807632896 | bytes 8519680 | tf_op jit(solution)/shard_map/mcb,bd->mcd/dot_general | solution.py:39
  116.7 4.0 %fusion.6 = (f32[32,128,128]{2,1,0:T(8,128)S(1)}, f32[32,128,128]{2,1,0:T(8,128)S(1)}) fusion(f32[32,128,128]{2,1,0:T(8,128)S(1)} %convolution_subtract_fusion.1, f32[8,128,128]{2,1,0:T(8,128)S(1)} %copy-done, f32[8,128,128]{2,1,0:T(8,128)S(1)} %copy-done.1, f32[32,128,128]{2,1,0:T(8,128)S(1)} %fusion.42, f32[32,128,128]{2,1,0:T(8,128)S(1)} %fusion.92, ...), kind=kOutput, calls=%fused_computation.14 | convolution fusion | flops 810778624 | bytes 13762560 | tf_op jit(solution)/shard_map/mcb,bd->mcd/dot_general | solution.py:42
  120.7 2.3 %fusion.62 = f32[32,128,128]{1,2,0:T(8,128)S(1)} fusion(f32[32,128,128]{2,1,0:T(8,128)S(1)} %get-tuple-element.128), kind=kOutput, calls=%fused_computation.143 | convolution fusion | flops 805535744 | bytes 4194304 | tf_op jit(solution)/shard_map/mcd,bd->mcb/dot_general | solution.py:50
  123.0 2.3 %fusion.60 = f32[32,128,128]{1,2,0:T(8,128)S(1)} fusion(f32[32,128,128]{2,1,0:T(8,128)S(1)} %get-tuple-element.127), kind=kOutput, calls=%fused_computation.141 | convolution fusion | flops 805535744 | bytes 4194304 | tf_op jit(solution)/shard_map/mcd,bd->mcb/dot_general | solution.py:53
  125.3 2.3 %convolution_add_fusion = f32[32,128,128]{1,2,0:T(8,128)S(1)} fusion(f32[32,128,128]{1,2,0:T(8,128)S(1)} %fusion.62, f32[32,128,128]{2,1,0:T(8,128)S(1)} %get-tuple-element.127), kind=kOutput, calls=%fused_computation.30 | convolution fusion | flops 806060032 | bytes 6291456 | tf_op jit(solution)/shard_map/mcd,bd->mcb/dot_general | solution.py:50
  127.5 2.5 %convolution_subtract_fusion = f32[32,128,128]{1,2,0:T(8,128)S(1)} fusion(f32[32,128,128]{1,2,0:T(8,128)S(1)} %fusion.60, f32[32,128,128]{2,1,0:T(8,128)S(1)} %get-tuple-element.128), kind=kOutput, calls=%fused_computation.29 | convolution fusion | flops 806060032 | bytes 6291456 | tf_op jit(solution)/shard_map/mcd,bd->mcb/dot_general | solution.py:53
  130.1 2.6 %fusion.9 = f32[32,128,64]{1,2,0:T(8,128)S(1)} fusion(f32[32,128,128]{1,2,0:T(8,128)S(1)} %convolution_add_fusion, f32[32,128,128]{1,2,0:T(8,128)S(1)} %convolution_subtract_fusion, f32[128,128]{0,1:T(8,128)S(1)} %get-tuple-element.132, f32[128,128]{0,1:T(8,128)S(1)} %get-tuple-element.133, f32[128,128]{0,1:T(8,128)S(1)} %fusion.77), kind=kOutput, calls=%fused_computation.21 | convolution fusion | flops 404226048 | bytes 5406720 | tf_op jit(solution)/shard_map/ca,mcb->mab/dot_general | solution.py:60
  132.7 3.6 %fusion.29 = f32[32,64,128]{2,1,0:T(8,128)} fusion(f32[32,128,64]{1,2,0:T(8,128)S(1)} %fusion.9, f32[32,128,128]{1,2,0:T(8,128)S(1)} %convolution_subtract_fusion, f32[32,128,128]{1,2,0:T(8,128)S(1)} %convolution_add_fusion, f32[128,128]{0,1:T(8,128)S(1)} %get-tuple-element.132, f32[128,128]{0,1:T(8,128)S(1)} %get-tuple-element.133, f32[128,128]{0,1:T(8,128)S(1)} %fusion.78), kind=kOutput, calls=%fused_computation.38 | convolution fusion | flops 405274624 | bytes 6455296 | tf_op jit(solution)/shard_map/ca,mcb->mab/dot_general | solution.py:58
  136.4 2.4 %reshape.154 = f32[1,4,8,8192]{3,2,1,0:T(8,128)} reshape(f32[32,64,128]{2,1,0:T(8,128)} %fusion.29) | data formatting | bytes 2097152 | tf_op jit(solution)/shard_map/convert_element_type | solution.py:171
  138.8 1.5 fusion.34
  141.2 20.9 %all_to_all.33 = bf16[64,1,4,8,128]{4,3,2,1,0:T(8,128)(2,1)S(1)} all-to-all(bf16[64,1,4,8,128]{4,3,2,1,0:T(8,128)(2,1)S(1)} %constant_dynamic-update-slice_fusion), channel_id=1, replica_groups=mesh['seq'=64,'mp'=4] {'seq'}, dimensions={0} | all-to-all | bytes 1048576 | tf_op jit(solution)/shard_map/all_to_all | solution.py:128
  162.2 23.2 %all_to_all.34 = bf16[64,4,8,128]{3,2,0,1:T(8,128)(2,1)S(1)} all-to-all(bf16[64,4,8,128]{3,2,0,1:T(8,128)(2,1)S(1)} %copy.284), channel_id=1, replica_groups=mesh['seq'=64,'mp'=4] {'mp'}, dimensions={1} | all-to-all | bytes 1048576 | tf_op jit(solution)/shard_map/all_to_all | solution.py:126
  185.4 0.9 copy.285
  (108 shorter events, 2.5 us)
Async XLA Ops:
  2.8 11.3 %copy-start.4 = (f32[32,16]{0,1:T(8,128)S(1)}, f32[32,16]{0,1:T(8,128)}, u32[]{:S(2)}) copy-start(f32[32,16]{0,1:T(8,128)} %param.11) | copy-start | bytes 6148
  2.8 11.3 %copy-start.5 = (f32[32,16]{0,1:T(8,128)S(1)}, f32[32,16]{0,1:T(8,128)}, u32[]{:S(2)}) copy-start(f32[32,16]{0,1:T(8,128)} %param.10) | copy-start | bytes 6148
  2.8 48.3 %all-to-all-start = ((bf16[3,64,4,8,128]{4,3,2,0,1:T(8,128)(2,1)}), bf16[3,64,4,8,128]{4,3,2,0,1:T(8,128)(2,1)S(1)}, u32[]{:S(2)}, u32[]{:S(2)}) async-start(bf16[3,64,4,8,128]{4,3,2,0,1:T(8,128)(2,1)} %copy.252), calls=%async_computation | async-start | bytes 3145728 | tf_op jit(solution)/shard_map/all_to_all | solution.py:112
  53.8 47.1 %all-to-all-start.1 = ((bf16[3,1,4,8,8192]{4,3,0,1,2:T(8,128)(2,1)}), bf16[3,1,4,8,8192]{4,3,0,1,2:T(8,128)(2,1)S(1)}, u32[]{:S(2)}, u32[]{:S(2)}) async-start(bf16[3,1,4,8,8192]{4,3,0,1,2:T(8,128)(2,1)} %reshape.170), calls=%async_computation.1 | async-start | bytes 3145728 | tf_op jit(solution)/shard_map/all_to_all | solution.py:111
  61.0 3.3 %copy-start.2 = (f32[3,3,8192]{2,1,0:T(4,128)S(1)}, f32[3,3,8192]{2,1,0:T(4,128)}, u32[]{:S(2)}) copy-start(f32[3,3,8192]{2,1,0:T(4,128)} %param.8) | copy-start | bytes 884740
  61.0 3.9 %copy-start.3 = (f32[8192]{0:T(1024)S(1)}, f32[8192]{0:T(1024)}, u32[]{:S(2)}) copy-start(f32[8192]{0:T(1024)} %param.9) | copy-start | bytes 98308
  113.0 3.7 %copy-start = (f32[8,128,128]{2,1,0:T(8,128)S(1)}, f32[8,128,128]{2,1,0:T(8,128)}, u32[]{:S(2)}) copy-start(f32[8,128,128]{2,1,0:T(8,128)} %convolution_add_fusion.2) | copy-start | bytes 1572868
  113.0 3.7 %copy-start.1 = (f32[8,128,128]{2,1,0:T(8,128)S(1)}, f32[8,128,128]{2,1,0:T(8,128)}, u32[]{:S(2)}) copy-start(f32[8,128,128]{2,1,0:T(8,128)} %convolution_subtract_fusion.2) | copy-start | bytes 1572868
